TPU v7x, 256 devices: a whole 4x4x8 slice. The times are simulated.
256 devices in a mesh: gx: 16 (over y, x), gy: 8 (over z), gz: 2 (over core).
Axes of the slice: x: 4, y: 4, z: 8, core: 2. Of those that a mesh axis runs over, the one named last changes fastest.
Arguments:
- tokens_in: bfloat16 [2048, 12288], P('gx', ('gz', 'gy')), may hold values from -20.4 to 20.4
- qkv_weight: bfloat16 [96, 128, 64, 384], P('gz', 'gx', 'gy'), may hold values from -0.0546875 to 0.0546875
- qkv_mask: int32 [96, 64, 3], P('gz', 'gy'), may hold values from 0 to 1, as said below
- out_weight: bfloat16 [64, 128, 12288], P('gy', 'gx', 'gz'), may hold values from -0.0625 to 0.0625
- out_mask: int32 [64, 96], P('gy', 'gz'), may hold values from 0 to 1, as said below
Outputs:
- mixed: bfloat16 [2048, 12288], P(('gx', 'gy'), 'gz')
Inputs may be any that keep to these rules, and one draw needn't show every extreme that they name: `qkv_mask`: exactly half of the blocks are kept within each face of 48 row blocks by 8 heads by 3 (row blocks r * 48 to r * 48 + 47, heads g * 8 to g * 8 + 7). `out_mask`: exactly half of the blocks are kept within each face of 8 heads by 48 column blocks, aligned as for qkv_mask.
All inputs are finite; a program needn't handle non-finite values.
Results may differ from a plain program's by a relative error of at most 0.005.
The roundings to bfloat16 on the way count: a program that leaves them out, or rounds other values in their place, can miss the bound.
Values may be sent and summed in bfloat16 or wider, within the bound.
No kernel may reach another device: no remote copies, remote signals or barrier semaphores. Data moves between devices by JAX's collectives and lax.ppermute only.
A program may use at most 192 MiB of HBM per device.

v0:
```python
import jax
import jax.numpy as jnp
from jax import lax
from jax.sharding import PartitionSpec as P

HEAD = 128
BLOCK = 128


def body(tokens_in, qkv_weight, qkv_mask, out_weight, out_mask):
    features = lax.all_gather(tokens_in, "gy", axis=1, tiled=True)
    tok_rows = features.shape[0]
    row_blocks, sub_rows, group_heads, triple = qkv_weight.shape
    full_tiles = lax.all_gather(qkv_weight, "gx", axis=1, tiled=True)
    keep_qkv = qkv_mask.astype(jnp.bfloat16)[:, None, :, :, None]
    masked = full_tiles.reshape(row_blocks, BLOCK, group_heads, 3, HEAD) * keep_qkv
    masked = masked.reshape(row_blocks * BLOCK, group_heads * triple)
    partial_value = jnp.dot(features, masked, preferred_element_type=jnp.float32)
    partial_value = partial_value.reshape(tok_rows, group_heads, triple)
    own_heads = lax.psum_scatter(partial_value, "gz", scatter_dimension=1, tiled=True).astype(
        jnp.bfloat16
    )
    queries = own_heads[:, :, :HEAD]
    keys_mine = own_heads[:, :, HEAD : 2 * HEAD]
    values_mine = own_heads[:, :, 2 * HEAD :]
    keys_all, values_all = (
        lax.all_gather(keys_mine, "gx", axis=0, tiled=True),
        lax.all_gather(values_mine, "gx", axis=0, tiled=True),
    )
    total_tokens = keys_all.shape[0]
    offset = lax.axis_index("gx") * tok_rows
    scores = jnp.einsum(
        "qhd,khd->hqk", queries, keys_all, preferred_element_type=jnp.float32
    ) * HEAD ** (-0.5)
    query_pos = offset + jnp.arange(tok_rows)
    key_pos = jnp.arange(total_tokens)
    allowed = key_pos[None, :] <= query_pos[:, None]
    scores = jnp.where(allowed[None], scores, -1e30)
    row_top = jnp.max(scores, axis=2, keepdims=True)
    weights = jnp.exp(scores - row_top)
    normed = (weights / jnp.sum(weights, axis=2, keepdims=True)).astype(jnp.bfloat16)
    attended = jnp.einsum(
        "hqk,khd->qhd", normed, values_all, preferred_element_type=jnp.float32
    ).astype(jnp.bfloat16)
    gathered = lax.all_gather(attended, "gz", axis=1, tiled=True)
    out_heads, out_sub, out_cols = out_weight.shape
    col_blocks = out_cols // BLOCK
    out_full = lax.all_gather(out_weight, "gx", axis=1, tiled=True)
    keep_out = out_mask.astype(jnp.bfloat16)[:, None, :, None]
    out_masked = out_full.reshape(out_heads, HEAD, col_blocks, BLOCK) * keep_out
    flat_in = gathered.reshape(tok_rows, out_heads * HEAD)
    summed = jnp.dot(
        flat_in, out_masked.reshape(out_heads * HEAD, out_cols), preferred_element_type=jnp.float32
    )
    return lax.psum_scatter(summed, "gy", scatter_dimension=0, tiled=True).astype(jnp.bfloat16)


def solution(mesh):
    return jax.shard_map(
        body,
        mesh=mesh,
        in_specs=(
            P("gx", ("gz", "gy")),
            P("gz", "gx", "gy", None),
            P("gz", "gy", None),
            P("gy", "gx", "gz"),
            P("gy", "gz"),
        ),
        out_specs=P(("gx", "gy"), "gz"),
        check_vma=False,
    )
```

profile of v0, /device:TPU:4, one launch (start us, length us, event | category | flops | bytes accessed | tf_op | source)
XLA Modules:
  0.0 631.0 jit_solution(10556620752532145886)
XLA Ops:
  6.5 0.7 all-gather.6.cloned.1.call-update
  7.3 0.7 all-gather.8.cloned.1.call-update
  8.1 0.7 convert_element_type.21
  8.8 227.4 %all-gather.6.cloned.1.call-done = bf16[48,128,8,384]{3,2,1,0:T(8,128)(2,1)} async-done(((bf16[48,8,8,384]{3,2,1,0:T(8,128)(2,1)}), bf16[48,128,8,384]{3,2,1,0:T(8,128)(2,1)}) %all-gather.6.cloned.1.call-update) | async-done | bytes 37748752 | tf_op jit(solution)/shard_map/all_gather | solution.py:14
  236.2 25.3 %copy.21 = bf16[768,8,8,384]{3,1,2,0:T(8,128)(2,1)} copy(bf16[768,8,8,384]{3,2,1,0:T(8,128)(2,1)} %bitcast.25) | data formatting | bytes 75497472
  261.4 48.7 %copy.20 = bf16[6144,3072]{0,1:T(8,128)(2,1)} copy(bf16[6144,3072]{1,0:T(8,128)(2,1)} %bitcast.23) | data formatting | bytes 75497472 | tf_op jit(solution)/shard_map/reshape | solution.py:16
  310.2 12.6 %mul.34 = bf16[48,128,8,3,128]{1,0,4,3,2:T(8,128)(2,1)} broadcast(bf16[48,8,3]{0,2,1:T(4,128)(2,1)S(1)} %copy.14), dimensions={0,2,3} | broadcast | bytes 37751040 | tf_op jit(solution)/shard_map/mul | solution.py:16
  322.8 26.7 %fusion.1 = f32[3072,128]{1,0:T(8,128)S(1)} fusion(bf16[128,6144]{1,0:T(8,128)(2,1)S(1)} %copy-done.1, bf16[6144,3072]{0,1:T(8,128)(2,1)} %copy.20, bf16[384,8,48,128]{3,2,1,0:T(8,128)(2,1)} %bitcast.24), kind=kOutput, calls=%fused_computation.2 | convolution fusion | flops 4850712576 | bytes 78643200 | tf_op jit(solution)/shard_map/dot_general | solution.py:18
  349.5 1.6 copy.15
  351.2 14.4 %reduce-scatter.3.cloned.1.call-done = f32[128,4,384]{2,0,1:T(8,128)} async-done(((f32[128,8,384]{2,0,1:T(8,128)}), f32[128,4,384]{2,0,1:T(8,128)}) %reduce-scatter.3.cloned.1.call-update) | async-done | bytes 786448 | tf_op jit(solution)/shard_map/reduce_scatter | solution.py:20
  365.6 1.2 convert_element_type.22
  366.8 0.7 fusion.26
  367.6 0.5 all-gather.10.cloned.1.call-update
  368.2 0.5 all-gather.14.cloned.1.call-update
  368.9 0.2 iota_compare_fusion
  369.2 49.0 %all-gather.12.cloned.1.call-done = bf16[2048,4,128]{2,0,1:T(8,128)(2,1)} async-done(((bf16[128,4,128]{2,0,1:T(8,128)(2,1)}), bf16[2048,4,128]{2,0,1:T(8,128)(2,1)}) %all-gather.12.cloned.1.call-update) | async-done | bytes 2097168 | tf_op jit(solution)/shard_map/all_gather | solution.py:27
  418.2 5.1 fusion.27
  423.3 46.6 %all-gather.10.cloned.1.call-done = bf16[2048,4,128]{2,0,1:T(8,128)(2,1)} async-done(((bf16[128,4,128]{2,0,1:T(8,128)(2,1)}), bf16[2048,4,128]{2,0,1:T(8,128)(2,1)}) %all-gather.10.cloned.1.call-update) | async-done | bytes 2097168 | tf_op jit(solution)/shard_map/all_gather | solution.py:28
  469.9 3.8 fusion.15
  473.8 2.0 all_gather.22
  475.8 91.5 %all-gather.14.cloned.1.call-done = bf16[8,128,6144]{2,1,0:T(8,128)(2,1)} async-done(((bf16[8,8,6144]{2,1,0:T(8,128)(2,1)}), bf16[8,128,6144]{2,1,0:T(8,128)(2,1)}) %all-gather.14.cloned.1.call-update) | async-done | bytes 12582928 | tf_op jit(solution)/shard_map/all_gather | solution.py:48
  567.3 8.0 %fusion.5 = f32[128,6144]{1,0:T(8,128)} fusion(bf16[128,8,128]{2,0,1:T(8,128)(2,1)S(1)} %all_gather.22, bf16[8,128,6144]{2,1,0:T(8,128)(2,1)} %all-gather.14.cloned.1.call-done, bf16[8,6144]{1,0:T(8,128)(2,1)S(1)} %broadcast_bitcast_fusion), kind=kOutput, calls=%fused_computation.6 | convolution fusion | flops 1616904192 | bytes 16089088 | tf_op jit(solution)/shard_map/dot_general | solution.py:52
  575.4 47.1 %reduce-scatter.5.cloned.1.call-done = f32[16,6144]{1,0:T(8,128)} async-done(((f32[128,6144]{1,0:T(8,128)}), f32[16,6144]{1,0:T(8,128)}) %reduce-scatter.5.cloned.1.call-update) | async-done | bytes 393232 | tf_op jit(solution)/shard_map/reduce_scatter | solution.py:55
  622.4 1.7 convert_element_type.27
  (21 shorter events, 0.7 us)
Async XLA Ops:
  6.5 229.6 %all-gather.6.cloned.1.call-start = ((), (), s32[]{:S(2)}) async-start(), calls=%async_computation.2 | async-start | bytes 40108032 | tf_op jit(solution)/shard_map/all_gather | solution.py:14
  7.3 302.9 %all-gather.8.cloned.1.call-start = ((), (), s32[]{:S(2)}) async-start(), calls=%async_computation.3 | async-start | bytes 1769472 | tf_op jit(solution)/shard_map/all_gather | solution.py:11
  8.0 357.6 %reduce-scatter.3.cloned.1.call-start = ((), (), s32[]{:S(2)}) async-start(), calls=%async_computation.4 | async-start | bytes 2359296 | tf_op jit(solution)/shard_map/reduce_scatter | solution.py:20
  310.2 12.6 %copy-start.1 = (bf16[128,6144]{1,0:T(8,128)(2,1)S(1)}, bf16[128,6144]{1,0:T(8,128)(2,1)}, u32[]{:S(2)}) copy-start(bf16[128,6144]{1,0:T(8,128)(2,1)} %all-gather.8.cloned.1.call-done) | copy-start | bytes 4718596
  349.5 19.3 %copy-start = (s32[8,48]{1,0:T(8,128)S(1)}, s32[8,48]{1,0:T(8,128)}, u32[]{:S(2)}) copy-start(s32[8,48]{1,0:T(8,128)} %param.9) | copy-start | bytes 4612
  351.2 67.1 %all-gather.12.cloned.1.call-start = ((), (), s32[]{:S(2)}) async-start(), calls=%async_computation.6 | async-start | bytes 2228224 | tf_op jit(solution)/shard_map/all_gather | solution.py:27
  367.5 102.3 %all-gather.10.cloned.1.call-start = ((), (), s32[]{:S(2)}) async-start(), calls=%async_computation.5 | async-start | bytes 2228224 | tf_op jit(solution)/shard_map/all_gather | solution.py:28
  368.1 199.2 %all-gather.14.cloned.1.call-start = ((), (), s32[]{:S(2)}) async-start(), calls=%async_computation.7 | async-start | bytes 13369344 | tf_op jit(solution)/shard_map/all_gather | solution.py:48
  368.7 253.7 %reduce-scatter.5.cloned.1.call-start = ((), (), s32[]{:S(2)}) async-start(), calls=%async_computation.8 | async-start | bytes 3538944 | tf_op jit(solution)/shard_map/reduce_scatter | solution.py:55
Sparse Core Ops, SparseCore 0:
  9.8 226.3 all-gather.5
  237.9 39.2 all-gather.7
  351.3 14.2 reduce-scatter.2
  367.9 50.2 all-gather.11
  420.5 49.3 all-gather.9
  472.1 95.1 all-gather.13
  575.5 46.9 reduce-scatter.4
where the time goes:
time: 632 us; the launch traced here: 631 us
  waiting for transfers between devices  478 us (76%)
  local copies, waits for them, and re-layouts  89.3 us (14%)
  matrix products  43.6 us (7%)
  between operations  13.6 us (2%)
    all_gather x1, waiting for transfers between devices, body(): full_tiles = lax.all_gather(qkv_weight, 'gx', axis=1, tiled=True)  227 us
    all_gather x1, waiting for transfers between devices, body(): out_full = lax.all_gather(out_weight, 'gx', axis=1, tiled=True)  91.5 us
    all_gather x1, waiting for transfers between devices, body(): lax.all_gather(keys_mine, 'gx', axis=0, tiled=True)  49 us
    reshape x1, local copies, waits for them, and re-layouts, body(): full_tiles.reshape(row_blocks, BLOCK, group_heads, 3, HEAD) * keep_qkv  48.7 us
    reduce_scatter x1, waiting for transfers between devices, body(): lax.psum_scatter(summed, 'gy', scatter_dimension=0, tiled=True)  47.1 us
    all_gather x1, waiting for transfers between devices, body(): lax.all_gather(values_mine, 'gx', axis=0, tiled=True)  46.6 us
    dot_general x1, matrix products, body(): jnp.dot(features, masked, preferred_element_type=jnp.float32)  26.7 us
    unnamed x5, local copies, waits for them, and re-layouts  25.3 us
  transfers between devices with their start and end apart: 7, of which 6 were waited for; matrix products, arithmetic and copies ran while one was open for 13% of the time, Pallas kernels for 0%

commit v1 on v0

--- a/solution.py
+++ b/solution.py
@@ -45,7 +45,9 @@
     gathered = lax.all_gather(attended, "gz", axis=1, tiled=True)
     out_heads, out_sub, out_cols = out_weight.shape
     col_blocks = out_cols // BLOCK
-    out_full = lax.all_gather(out_weight, "gx", axis=1, tiled=True)
+    out_full = jnp.concatenate(
+        lax.all_to_all(jnp.stack([out_weight] * lax.axis_size("gx")), "gx", 0, 0), axis=1
+    )
     keep_out = out_mask.astype(jnp.bfloat16)[:, None, :, None]
     out_masked = out_full.reshape(out_heads, HEAD, col_blocks, BLOCK) * keep_out
     flat_in = gathered.reshape(tok_rows, out_heads * HEAD)

time: 632 us -> 691 us (1.093)
  waiting for transfers between devices: 478 us -> 512 us
  other arithmetic: 3.81 us -> 13.6 us
  local copies, waits for them, and re-layouts: 89.3 us -> 97 us
  starting transfers between devices: 0.24 us -> 7.78 us
    all_gather x1, waiting for transfers between devices: 227 us -> 358 us  [body(): full_tiles = lax.all_gather(qkv_weight, 'gx', axis=1, tiled=True)]
    all_gather x1 -> x0, waiting for transfers between devices: 91.5 us -> none  [body(): out_full = lax.all_gather(out_weight, 'gx', axis=1, tiled=True)]
    mul x0 -> x1, other arithmetic: none -> 10.5 us  [body(): out_masked = out_full.reshape(out_heads, HEAD, col_blocks, BLOCK) * keep_out]
    all_gather x1, waiting for transfers between devices: 49 us -> 39.1 us  [body(): lax.all_gather(keys_mine, 'gx', axis=0, tiled=True)]
    all_to_all x0 -> x1, starting transfers between devices: none -> 7.58 us  [body(): lax.all_to_all(jnp.stack([out_weight] * lax.axis_size('gx')), 'gx', 0, 0)]
    another operation x0 -> x1, local copies, waits for them, and re-layouts: none -> 7.32 us  [body(): jnp.stack([out_weight] * lax.axis_size('gx'))]
    unnamed x5 -> x7, local copies, waits for them, and re-layouts: 25.3 us -> 25.4 us
  transfers between devices with their start and end apart: 7 -> 7, of which waited for: 6 -> 5; matrix products, arithmetic and copies ran while one was open for 13% -> 20% of each run, Pallas kernels for 0% -> 0%
where the time goes in v1:
time: 691 us; the launch traced here: 689 us
  waiting for transfers between devices  512 us (74%)
  local copies, waits for them, and re-layouts  97 us (14%)
  matrix products  43.6 us (6%)
  other arithmetic  13.6 us (2%)
  between operations  13.6 us (2%)
  starting transfers between devices  7.78 us (1%)
    all_gather x1, waiting for transfers between devices, body(): full_tiles = lax.all_gather(qkv_weight, 'gx', axis=1, tiled=True)  358 us
    reshape x1, local copies, waits for them, and re-layouts, body(): full_tiles.reshape(row_blocks, BLOCK, group_heads, 3, HEAD) * keep_qkv  48.7 us
    reduce_scatter x1, waiting for transfers between devices, body(): lax.psum_scatter(summed, 'gy', scatter_dimension=0, tiled=True)  47.6 us
    all_gather x1, waiting for transfers between devices, body(): lax.all_gather(values_mine, 'gx', axis=0, tiled=True)  46.6 us
    all_gather x1, waiting for transfers between devices, body(): lax.all_gather(keys_mine, 'gx', axis=0, tiled=True)  39.1 us
    dot_general x1, matrix products, body(): jnp.dot(features, masked, preferred_element_type=jnp.float32)  26.7 us
    unnamed x7, local copies, waits for them, and re-layouts  25.4 us
    reduce_scatter x1, waiting for transfers between devices, body(): lax.psum_scatter(partial_value, 'gz', scatter_dimension=1, tiled=True)  18.3 us
  transfers between devices with their start and end apart: 7, of which 5 were waited for; matrix products, arithmetic and copies ran while one was open for 20% of the time, Pallas kernels for 0%

profile of v1, /device:TPU:4, one launch (start us, length us, event | category | flops | bytes accessed | tf_op | source)
XLA Modules:
  0.0 689.2 jit_solution(16229127853399805226)
XLA Ops:
  6.5 0.7 all-gather.5.cloned.1.call-update
  7.3 0.7 all-gather.7.cloned.1.call-update
  8.0 7.3 %stack.2 = bf16[16,8,8,6144]{3,2,1,0:T(8,128)(2,1)} broadcast(bf16[8,8,6144]{2,1,0:T(8,128)(2,1)} %param.8), dimensions={1,2,3} | broadcast | bytes 13369344 | tf_op jit(solution)/shard_map/stack | solution.py:49
  15.3 7.6 %all-to-all-start = ((bf16[16,8,8,6144]{3,2,1,0:T(8,128)(2,1)}), bf16[16,8,8,6144]{3,2,1,0:T(8,128)(2,1)}, u32[]{:S(2)}, u32[]{:S(2)}) async-start(bf16[16,8,8,6144]{3,2,1,0:T(8,128)(2,1)} %stack.2), calls=%async_computation.1 | async-start | bytes 25165824 | tf_op jit(solution)/shard_map/all_to_all | solution.py:49
  23.0 358.1 %all-gather.5.cloned.1.call-done = bf16[48,128,8,384]{3,2,1,0:T(8,128)(2,1)} async-done(((bf16[48,8,8,384]{3,2,1,0:T(8,128)(2,1)}), bf16[48,128,8,384]{3,2,1,0:T(8,128)(2,1)}) %all-gather.5.cloned.1.call-update) | async-done | bytes 37748752 | tf_op jit(solution)/shard_map/all_gather | solution.py:14
  381.1 25.4 %copy.32 = bf16[768,8,8,384]{3,1,2,0:T(8,128)(2,1)} copy(bf16[768,8,8,384]{3,2,1,0:T(8,128)(2,1)} %bitcast.29) | data formatting | bytes 75497472
  406.5 48.7 %copy.31 = bf16[6144,3072]{0,1:T(8,128)(2,1)} copy(bf16[6144,3072]{1,0:T(8,128)(2,1)} %bitcast.26) | data formatting | bytes 75497472 | tf_op jit(solution)/shard_map/reshape | solution.py:16
  455.2 12.6 %mul.39 = bf16[48,128,8,3,128]{1,0,4,3,2:T(8,128)(2,1)} broadcast(bf16[48,8,3]{0,2,1:T(4,128)(2,1)S(1)} %copy.23), dimensions={0,2,3} | broadcast | bytes 37751040 | tf_op jit(solution)/shard_map/mul | solution.py:16
  467.8 26.7 %fusion.1 = f32[3072,128]{1,0:T(8,128)S(1)} fusion(bf16[128,6144]{1,0:T(8,128)(2,1)S(1)} %copy-done.2, bf16[6144,3072]{0,1:T(8,128)(2,1)} %copy.31, bf16[384,8,48,128]{3,2,1,0:T(8,128)(2,1)} %bitcast.28), kind=kOutput, calls=%fused_computation.2 | convolution fusion | flops 4850712576 | bytes 78643200 | tf_op jit(solution)/shard_map/dot_general | solution.py:18
  494.5 1.6 copy.24
  496.2 18.3 %reduce-scatter.3.cloned.1.call-done = f32[128,4,384]{2,0,1:T(8,128)} async-done(((f32[128,8,384]{2,0,1:T(8,128)}), f32[128,4,384]{2,0,1:T(8,128)}) %reduce-scatter.3.cloned.1.call-update) | async-done | bytes 786448 | tf_op jit(solution)/shard_map/reduce_scatter | solution.py:20
  514.5 1.2 convert_element_type.22
  515.7 0.7 fusion.20
  516.5 0.5 all-gather.9.cloned.1.call-update
  517.1 0.2 iota_compare_fusion
  517.6 10.5 %copy_multiply_fusion = bf16[16,8,8,6144]{3,2,0,1:T(8,128)(2,1)} fusion(bf16[16,8,8,6144]{3,2,1,0:T(8,128)(2,1)} %all-to-all-done, bf16[8,6144]{1,0:T(8,128)(2,1)S(1)} %broadcast_bitcast_fusion), kind=kLoop, calls=%fused_computation.4 | loop fusion | flops 6291456 | bytes 25264128 | tf_op jit(solution)/shard_map/mul | solution.py:52
  528.1 39.1 %all-gather.11.cloned.1.call-done = bf16[2048,4,128]{2,0,1:T(8,128)(2,1)} async-done(((bf16[128,4,128]{2,0,1:T(8,128)(2,1)}), bf16[2048,4,128]{2,0,1:T(8,128)(2,1)}) %all-gather.11.cloned.1.call-update) | async-done | bytes 2097168 | tf_op jit(solution)/shard_map/all_gather | solution.py:27
  567.2 5.1 fusion.21
  572.2 46.6 %all-gather.9.cloned.1.call-done = bf16[2048,4,128]{2,0,1:T(8,128)(2,1)} async-done(((bf16[128,4,128]{2,0,1:T(8,128)(2,1)}), bf16[2048,4,128]{2,0,1:T(8,128)(2,1)}) %all-gather.9.cloned.1.call-update) | async-done | bytes 2097168 | tf_op jit(solution)/shard_map/all_gather | solution.py:28
  618.8 3.8 fusion.9
  622.7 2.0 all_gather.19
  624.9 8.1 %fusion.24 = f32[128,6144]{1,0:T(8,128)} fusion(bf16[128,1024]{0,1:T(8,128)(2,1)S(1)} %bitcast.31, bf16[1024,6144]{1,0:T(8,128)(2,1)} %bitcast.27), kind=kOutput, calls=%fused_computation.26 | convolution fusion | flops 1610612736 | bytes 15990784 | tf_op jit(solution)/shard_map/dot_general | solution.py:54
  633.0 47.6 %reduce-scatter.5.cloned.1.call-done = f32[16,6144]{1,0:T(8,128)} async-done(((f32[128,6144]{1,0:T(8,128)}), f32[16,6144]{1,0:T(8,128)}) %reduce-scatter.5.cloned.1.call-update) | async-done | bytes 393232 | tf_op jit(solution)/shard_map/reduce_scatter | solution.py:57
  680.6 1.7 convert_element_type.27
  (25 shorter events, 0.8 us)
Async XLA Ops:
  6.5 374.5 %all-gather.5.cloned.1.call-start = ((), (), s32[]{:S(2)}) async-start(), calls=%async_computation.3 | async-start | bytes 40108032 | tf_op jit(solution)/shard_map/all_gather | solution.py:14
  7.3 448.0 %all-gather.7.cloned.1.call-start = ((), (), s32[]{:S(2)}) async-start(), calls=%async_computation.4 | async-start | bytes 1769472 | tf_op jit(solution)/shard_map/all_gather | solution.py:11
  15.3 7.6 %copy-start = (s32[48,8,3]{0,1,2:T(8,128)S(1)}, s32[48,8,3]{0,1,2:T(8,128)}, u32[]{:S(2)}) copy-start(s32[48,8,3]{0,1,2:T(8,128)} %param.7) | copy-start | bytes 13828
  15.3 502.2 %all-to-all-start = ((bf16[16,8,8,6144]{3,2,1,0:T(8,128)(2,1)}), bf16[16,8,8,6144]{3,2,1,0:T(8,128)(2,1)}, u32[]{:S(2)}, u32[]{:S(2)}) async-start(bf16[16,8,8,6144]{3,2,1,0:T(8,128)(2,1)} %stack.2), calls=%async_computation.1 | async-start | bytes 25165824 | tf_op jit(solution)/shard_map/all_to_all | solution.py:49
  22.9 491.6 %reduce-scatter.3.cloned.1.call-start = ((), (), s32[]{:S(2)}) async-start(), calls=%async_computation.5 | async-start | bytes 2359296 | tf_op jit(solution)/shard_map/reduce_scatter | solution.py:20
  455.2 12.6 %copy-start.2 = (bf16[128,6144]{1,0:T(8,128)(2,1)S(1)}, bf16[128,6144]{1,0:T(8,128)(2,1)}, u32[]{:S(2)}) copy-start(bf16[128,6144]{1,0:T(8,128)(2,1)} %all-gather.7.cloned.1.call-done) | copy-start | bytes 4718596
  494.5 22.8 %copy-start.1 = (s32[8,48]{1,0:T(8,128)S(1)}, s32[8,48]{1,0:T(8,128)}, u32[]{:S(2)}) copy-start(s32[8,48]{1,0:T(8,128)} %param.9) | copy-start | bytes 4612
  496.2 71.0 %all-gather.11.cloned.1.call-start = ((), (), s32[]{:S(2)}) async-start(), calls=%async_computation.7 | async-start | bytes 2228224 | tf_op jit(solution)/shard_map/all_gather | solution.py:27
  516.5 102.3 %all-gather.9.cloned.1.call-start = ((), (), s32[]{:S(2)}) async-start(), calls=%async_computation.6 | async-start | bytes 2228224 | tf_op jit(solution)/shard_map/all_gather | solution.py:28
  517.1 163.6 %reduce-scatter.5.cloned.1.call-start = ((), (), s32[]{:S(2)}) async-start(), calls=%async_computation.8 | async-start | bytes 3538944 | tf_op jit(solution)/shard_map/reduce_scatter | solution.py:57
Sparse Core Ops, SparseCore 0:
  9.8 371.2 all-gather.4
  382.9 43.1 all-gather.6
  496.3 18.1 reduce-scatter.2
  516.8 50.2 all-gather.10
  569.4 49.3 all-gather.8
  633.1 47.4 reduce-scatter.4
